TPU v7x, 256 devices: a whole 4x4x8 slice. The times are simulated.
256 devices in a mesh: tm: 4 (over z_hi, core), height: 16 (over x, y), width: 4 (over z_lo).
Axes of the slice: x: 4, y: 4, z: 8 (z_hi: 2, z_lo: 4; z = z_hi * 4 + z_lo), core: 2. Of those that a mesh axis runs over, the one named last changes fastest.
Arguments:
- frames: bfloat16 [8, 64, 128, 384], P('tm', 'height', 'width'), may hold values from -6 to 6
- cache_in: bfloat16 [2, 64, 128, 384], P(None, 'height', 'width'), may hold values from -6 to 6
- kernel: bfloat16 [384, 3, 3, 3, 384], replicated, may hold values from -0.0625 to 0.0625
- conv_bias: float32 [384], replicated, may hold values from -3 to 3
- cotangent: bfloat16 [8, 64, 128, 384], P('tm', 'height', 'width'), may hold values from -6 to 6
Outputs:
- decoded: bfloat16 [8, 64, 128, 384], P('tm', 'height', 'width')
- frame_grad: bfloat16 [8, 64, 128, 384], P('tm', 'height', 'width')
- cache_grad: bfloat16 [8, 64, 128, 384], P('tm', 'height', 'width')
- kernel_grad: float32 [384, 3, 3, 3, 384], P('height')
All inputs are finite; a program needn't handle non-finite values.
Results may differ from a plain program's by a relative error of at most 0.0053.
Values may be sent and summed in bfloat16 or wider, within the bound.
No kernel may reach another device: no remote copies, remote signals or barrier semaphores. Data moves between devices by JAX's collectives and lax.ppermute only.
A program may use at most 256 MiB of HBM per device.

v0:
```python
import jax
import jax.numpy as jnp
from jax import lax
from jax.sharding import PartitionSpec as P


def shifted(value, axis, by):
    length = lax.axis_size(axis)
    pairs = [(i, i + by) for i in range(length) if 0 <= i + by < length]
    return lax.ppermute(value, axis, pairs)


def with_halo(value, sides, width):
    for axis, dim in sides:
        size, length = (lax.axis_size(axis), value.shape[dim])
        up = [(i, (i + 1) % size) for i in range(size - 1)]
        down = [(j, i) for i, j in up]
        last = lax.slice_in_dim(value, length - width, length, axis=dim)
        initial = lax.slice_in_dim(value, 0, width, axis=dim)
        before = lax.ppermute(last, axis, up)
        after = lax.ppermute(initial, axis, down)
        value = jnp.concatenate([before, value, after], axis=dim)
    return value


def tap_block(padded, tap_t, tap_h, tap_w, depth_count, row_count, col_count):
    block = padded[
        tap_t : tap_t + depth_count, tap_h : tap_h + row_count, tap_w : tap_w + col_count
    ]
    return block.reshape(-1, block.shape[-1])


def body(frames, cache_in, kernel, conv_bias, cotangent):
    frame_count, row_count, col_count, channels = frames.shape
    is_first = lax.axis_index("tm") == 0
    earlier = shifted(frames, "tm", 1)
    earlier = jnp.where(is_first, cache_in, earlier)
    stacked = jnp.concatenate([earlier, frames], 0)
    extended = with_halo(stacked, (("height", 1), ("width", 2)), 1)
    pre_act = jnp.zeros((frame_count * row_count * col_count, channels), jnp.float32) + conv_bias
    for tap_t in range(3):
        for tap_h in range(3):
            for tap_w in range(3):
                block = tap_block(extended, tap_t, tap_h, tap_w, frame_count, row_count, col_count)
                pre_act = pre_act + lax.dot_general(
                    block,
                    kernel[:, tap_t, tap_h, tap_w, :],
                    (((1,), (1,)), ((), ())),
                    preferred_element_type=jnp.float32,
                )
    sigma = jax.nn.sigmoid(pre_act)
    decoded = (pre_act * sigma).astype(jnp.bfloat16).reshape(frames.shape)
    scaled = (
        cotangent.reshape(-1, channels).astype(jnp.float32)
        * sigma
        * (1.0 + pre_act * (1.0 - sigma))
    ).astype(jnp.bfloat16)
    grad_rimmed = with_halo(scaled.reshape(frames.shape), (("height", 1), ("width", 2)), 1)
    partial_value = jnp.zeros((frame_count + 2, row_count, col_count, channels), jnp.float32)
    for tap_t in range(3):
        contrib = jnp.zeros((frame_count * row_count * col_count, channels), jnp.float32)
        for tap_h in range(3):
            for tap_w in range(3):
                block = grad_rimmed[
                    :, 2 - tap_h : 2 - tap_h + row_count, 2 - tap_w : 2 - tap_w + col_count
                ].reshape(-1, channels)
                contrib = contrib + jnp.dot(
                    block, kernel[:, tap_t, tap_h, tap_w, :], preferred_element_type=jnp.float32
                )
        partial_value = partial_value.at[tap_t : tap_t + frame_count].add(
            contrib.reshape(frame_count, row_count, col_count, channels)
        )
    cache_grad = partial_value[:2].astype(jnp.bfloat16)
    carried = shifted(cache_grad, "tm", -1)
    frame_grad = (
        partial_value[2:]
        .at[frame_count - 2 :]
        .add(carried.astype(jnp.float32))
        .astype(jnp.bfloat16)
    )
    pieces = []
    for tap_t in range(3):
        for tap_h in range(3):
            for tap_w in range(3):
                block = tap_block(extended, tap_t, tap_h, tap_w, frame_count, row_count, col_count)
                pieces.append(
                    lax.dot_general(
                        scaled, block, (((0,), (0,)), ((), ())), preferred_element_type=jnp.float32
                    )
                )
    owned = lax.psum_scatter(
        jnp.stack(pieces, 1).reshape(
            channels // lax.axis_size("height") * lax.axis_size("height"), 3, 3, 3, channels
        ),
        "height",
        scatter_dimension=0,
        tiled=True,
    )
    kernel_grad = lax.psum(owned, ("tm", "width"))
    return (decoded, frame_grad, cache_grad, kernel_grad)


def solution(mesh):
    in_specs = (
        P("tm", "height", "width", None),
        P(None, "height", "width", None),
        P(),
        P(),
        P("tm", "height", "width", None),
    )
    out_specs = (
        P("tm", "height", "width", None),
        P("tm", "height", "width", None),
        P("tm", "height", "width", None),
        P("height", None, None, None, None),
    )
    return jax.shard_map(body, mesh=mesh, in_specs=in_specs, out_specs=out_specs, check_vma=False)
```

profile of v0, /device:TPU:1, one launch (start us, length us, event | category | flops | bytes accessed | tf_op | source)
XLA Modules:
  0.0 323.4 jit_solution(16105572426888722058)
XLA Ops:
  7.2 10.2 %collective-permute-start = (bf16[2,4,32,384]{3,2,1,0:T(8,128)(2,1)}, bf16[2,4,32,384]{3,2,1,0:T(8,128)(2,1)S(1)}, u32[]{:S(2)}, u32[]{:S(2)}) collective-permute-start(bf16[2,4,32,384]{3,2,1,0:T(8,128)(2,1)} %param.15), channel_id=1, source_target_pairs={{0,64},{64,128},{128,192},{1,65},{65,129},{129,193},{2,66},{66,130... | collective-permute-start | bytes 589832 | tf_op jit(solution)/shard_map/ppermute | solution.py:10
  17.4 2.9 collective-permute-done
  21.2 3.2 collective-permute-start.1
  24.4 1.3 collective-permute-start.2
  26.7 3.1 collective-permute-done.2
  30.7 4.8 %collective-permute-start.3 = (bf16[4,6,1,384]{3,2,1,0:T(2,128)(2,1)S(1)}, bf16[4,6,1,384]{3,2,1,0:T(2,128)(2,1)S(1)}, u32[]{:S(2)}, u32[]{:S(2)}) collective-permute-start(bf16[4,6,1,384]{3,2,1,0:T(2,128)(2,1)S(1)} %get-tuple-element.80), channel_id=1, source_target_pairs={{0,1},{1,2},{2,3},{4,5},{5,6},{6,7},{8,9},{9,10},{10,11},{12,13},{... | collective-permute-start | bytes 55304 | tf_op jit(solution)/shard_map/ppermute | solution.py:20
  35.5 1.3 collective-permute-start.4
  36.8 1.1 pad_maximum_fusion.1
  38.1 2.1 collective-permute-done.4
  40.2 1.4 maximum_maximum_fusion
  52.0 1.1 fusion.25
  53.1 1.1 fusion.24
  54.3 1.1 fusion.23
  55.4 1.1 fusion.22
  56.5 1.1 fusion.21
  57.6 1.1 fusion.20
  58.7 1.1 fusion.19
  59.8 1.1 fusion.18
  62.1 1.1 fusion.16
  65.4 1.2 fusion.13
  66.6 1.2 fusion.12
  70.0 1.1 fusion.9
  71.1 1.1 fusion.8
  72.2 1.1 fusion.7
  73.3 1.1 fusion.6
  74.4 1.2 fusion.5
  77.8 1.1 fusion.2
  78.9 1.1 fusion.1
  80.0 1.1 fusion
  81.3 3.5 %collective-permute-start.5 = (bf16[2,1,32,384]{3,2,1,0:T(8,128)(2,1)S(1)}, bf16[2,1,32,384]{3,2,1,0:T(8,128)(2,1)S(1)}, u32[]{:S(2)}, u32[]{:S(2)}) collective-permute-start(bf16[2,1,32,384]{3,2,1,0:T(8,128)(2,1)S(1)} %get-tuple-element.106), channel_id=1, source_target_pairs={{0,4},{4,8},{8,12},{12,16},{16,20},{20,24},{24,28},{28,32},{32,36}... | collective-permute-start | bytes 147464 | tf_op jit(solution)/shard_map/ppermute | solution.py:20
  84.7 1.3 collective-permute-start.6
  86.1 3.5 %collective-permute-done.6 = bf16[2,1,32,384]{3,2,1,0:T(8,128)(2,1)S(1)} collective-permute-done((bf16[2,1,32,384]{3,2,1,0:T(8,128)(2,1)S(1)}, bf16[2,1,32,384]{3,2,1,0:T(8,128)(2,1)S(1)}, u32[]{:S(2)}, u32[]{:S(2)}) %collective-permute-start.6) | collective-permute-done | bytes 49184 | tf_op jit(solution)/shard_map/ppermute | solution.py:21
  89.6 1.3 collective-permute-start.7
  90.9 4.2 %collective-permute-start.8 = (bf16[2,6,1,384]{3,2,1,0:T(2,128)(2,1)S(1)}, bf16[2,6,1,384]{3,2,1,0:T(2,128)(2,1)S(1)}, u32[]{:S(2)}, u32[]{:S(2)}) collective-permute-start(bf16[2,6,1,384]{3,2,1,0:T(2,128)(2,1)S(1)} %get-tuple-element.103), channel_id=1, source_target_pairs={{0,1},{1,2},{2,3},{4,5},{5,6},{6,7},{8,9},{9,10},{10,11},{12,13},{... | collective-permute-start | bytes 27656 | tf_op jit(solution)/shard_map/ppermute | solution.py:20
  95.1 1.2 fusion.70
  96.4 1.2 fusion.91
  97.6 1.2 fusion.50
  99.2 1.5 fusion.75
  100.7 1.3 convolution_add_fusion.20
  102.0 1.2 convolution_add_fusion.19
  103.3 1.2 convolution_add_fusion.18
  104.5 1.2 convolution_add_fusion.17
  105.8 1.2 convolution_add_fusion.16
  110.0 1.9 collective-permute-start.9
  113.9 87.3 %reduce-scatter.2.cloned.1.call-done = f32[24,3,3,3,384]{4,0,3,2,1:T(8,128)} async-done(((f32[384,3,3,3,384]{4,0,3,2,1:T(8,128)}), f32[24,3,3,3,384]{4,0,3,2,1:T(8,128)}) %reduce-scatter.2.cloned.1.call-update) | async-done | bytes 995344 | tf_op jit(solution)/shard_map/reduce_scatter | solution.py:91
  201.2 1.2 fusion.30
  203.2 111.2 %all-reduce.3.cloned.1.call-done = f32[24,3,3,3,384]{4,0,3,2,1:T(8,128)} async-done(((f32[24,3,3,3,384]{4,0,3,2,1:T(8,128)}), f32[24,3,3,3,384]{4,0,3,2,1:T(8,128)}) %all-reduce.3.cloned.1.call-update) | async-done | bytes 995344 | tf_op jit(solution)/shard_map/psum | solution.py:99
  314.3 2.2 copy.37
  (96 shorter events, 26.7 us)
Async XLA Ops:
  7.2 194.0 %reduce-scatter.2.cloned.1.call-start = ((), (), s32[]{:S(2)}) async-start(), calls=%async_computation.1 | async-start | bytes 16920576 | tf_op jit(solution)/shard_map/reduce_scatter | solution.py:91
  7.2 13.1 %collective-permute-start = (bf16[2,4,32,384]{3,2,1,0:T(8,128)(2,1)}, bf16[2,4,32,384]{3,2,1,0:T(8,128)(2,1)S(1)}, u32[]{:S(2)}, u32[]{:S(2)}) collective-permute-start(bf16[2,4,32,384]{3,2,1,0:T(8,128)(2,1)} %param.15), channel_id=1, source_target_pairs={{0,64},{64,128},{128,192},{1,65},{65,129},{129,193},{2,66},{66,130... | collective-permute-start | bytes 589832 | tf_op jit(solution)/shard_map/ppermute | solution.py:10
  17.4 24.6 %slice-start = ((s8[7962624]{0:T(1024)(128)(4,1)}), s8[4194304]{0:T(1024)(128)(4,1)S(1)}, s32[]{:S(2)}) async-start(s8[7962624]{0:T(1024)(128)(4,1)} %bitcast.401), calls=%async_computation.3 | async-start | bytes 8388608
  20.4 22.0 %copy-start.2 = (f32[384]{0:T(512)S(1)}, f32[384]{0:T(512)}, u32[]{:S(2)}) copy-start(f32[384]{0:T(512)} %param.18) | copy-start | bytes 4612
  21.2 5.4 %collective-permute-start.1 = (bf16[4,1,32,384]{3,2,1,0:T(8,128)(2,1)S(1)}, bf16[4,1,32,384]{3,2,1,0:T(8,128)(2,1)S(1)}, u32[]{:S(2)}, u32[]{:S(2)}) collective-permute-start(bf16[4,1,32,384]{3,2,1,0:T(8,128)(2,1)S(1)} %get-tuple-element.92), channel_id=1, source_target_pairs={{0,4},{4,8},{8,12},{12,16},{16,20},{20,24},{24,28},{28,32},{32,36}... | collective-permute-start | bytes 294920 | tf_op jit(solution)/shard_map/ppermute | solution.py:20
  24.4 5.4 %collective-permute-start.2 = (bf16[4,1,32,384]{3,2,1,0:T(8,128)(2,1)S(1)}, bf16[4,1,32,384]{3,2,1,0:T(8,128)(2,1)S(1)}, u32[]{:S(2)}, u32[]{:S(2)}) collective-permute-start(bf16[4,1,32,384]{3,2,1,0:T(8,128)(2,1)S(1)} %get-tuple-element.93), channel_id=1, source_target_pairs={{4,0},{8,4},{12,8},{16,12},{20,16},{24,20},{28,24},{32,28},{36,32}... | collective-permute-start | bytes 294920 | tf_op jit(solution)/shard_map/ppermute | solution.py:21
  30.7 7.4 %collective-permute-start.3 = (bf16[4,6,1,384]{3,2,1,0:T(2,128)(2,1)S(1)}, bf16[4,6,1,384]{3,2,1,0:T(2,128)(2,1)S(1)}, u32[]{:S(2)}, u32[]{:S(2)}) collective-permute-start(bf16[4,6,1,384]{3,2,1,0:T(2,128)(2,1)S(1)} %get-tuple-element.80), channel_id=1, source_target_pairs={{0,1},{1,2},{2,3},{4,5},{5,6},{6,7},{8,9},{9,10},{10,11},{12,13},{... | collective-permute-start | bytes 55304 | tf_op jit(solution)/shard_map/ppermute | solution.py:20
  35.5 4.7 %collective-permute-start.4 = (bf16[4,6,1,384]{3,2,1,0:T(2,128)(2,1)S(1)}, bf16[4,6,1,384]{3,2,1,0:T(2,128)(2,1)S(1)}, u32[]{:S(2)}, u32[]{:S(2)}) collective-permute-start(bf16[4,6,1,384]{3,2,1,0:T(2,128)(2,1)S(1)} %get-tuple-element.81), channel_id=1, source_target_pairs={{1,0},{2,1},{3,2},{5,4},{6,5},{7,6},{9,8},{10,9},{11,10},{13,12},{... | collective-permute-start | bytes 55304 | tf_op jit(solution)/shard_map/ppermute | solution.py:21
  38.1 4.0 %slice-start.1 = ((s8[7962624]{0:T(1024)(128)(4,1)}), s8[3768320]{0:T(1024)(128)(4,1)S(1)}, s32[]{:S(2)}) async-start(s8[7962624]{0:T(1024)(128)(4,1)} %bitcast.401), calls=%async_computation.4 | async-start | bytes 7536640
  45.0 3.6 %copy-start = (bf16[2,4,32,384]{3,2,1,0:T(8,128)(2,1)S(1)}, bf16[2,4,32,384]{3,2,1,0:T(8,128)(2,1)}, u32[]{:S(2)}) copy-start(bf16[2,4,32,384]{3,2,1,0:T(8,128)(2,1)} %param.15) | copy-start | bytes 589828
  46.2 3.6 %copy-start.3 = (bf16[2,4,32,384]{3,2,1,0:T(8,128)(2,1)S(1)}, bf16[2,4,32,384]{3,2,1,0:T(8,128)(2,1)}, u32[]{:S(2)}) copy-start(bf16[2,4,32,384]{3,2,1,0:T(8,128)(2,1)} %param.19) | copy-start | bytes 589828
  81.2 233.1 %all-reduce.3.cloned.1.call-start = ((), (), s32[]{:S(2)}) async-start(), calls=%async_computation.2 | async-start | bytes 1990656 | tf_op jit(solution)/shard_map/psum | solution.py:99
  81.2 25.8 %slice-start.2 = ((s8[7962624]{0:T(1024)(128)(4,1)}), s8[3768320]{0:T(1024)(128)(4,1)S(1)}, s32[]{:S(2)}) async-start(s8[7962624]{0:T(1024)(128)(4,1)} %bitcast.403), calls=%async_computation.5 | async-start | bytes 7536640
  81.3 4.8 %collective-permute-start.5 = (bf16[2,1,32,384]{3,2,1,0:T(8,128)(2,1)S(1)}, bf16[2,1,32,384]{3,2,1,0:T(8,128)(2,1)S(1)}, u32[]{:S(2)}, u32[]{:S(2)}) collective-permute-start(bf16[2,1,32,384]{3,2,1,0:T(8,128)(2,1)S(1)} %get-tuple-element.106), channel_id=1, source_target_pairs={{0,4},{4,8},{8,12},{12,16},{16,20},{20,24},{24,28},{28,32},{32,36}... | collective-permute-start | bytes 147464 | tf_op jit(solution)/shard_map/ppermute | solution.py:20
  84.7 4.8 %collective-permute-start.6 = (bf16[2,1,32,384]{3,2,1,0:T(8,128)(2,1)S(1)}, bf16[2,1,32,384]{3,2,1,0:T(8,128)(2,1)S(1)}, u32[]{:S(2)}, u32[]{:S(2)}) collective-permute-start(bf16[2,1,32,384]{3,2,1,0:T(8,128)(2,1)S(1)} %get-tuple-element.107), channel_id=1, source_target_pairs={{4,0},{8,4},{12,8},{16,12},{20,16},{24,20},{28,24},{32,28},{36,32}... | collective-permute-start | bytes 147464 | tf_op jit(solution)/shard_map/ppermute | solution.py:21
  89.6 9.2 %collective-permute-start.7 = (bf16[2,6,1,384]{3,2,1,0:T(2,128)(2,1)S(1)}, bf16[2,6,1,384]{3,2,1,0:T(2,128)(2,1)S(1)}, u32[]{:S(2)}, u32[]{:S(2)}) collective-permute-start(bf16[2,6,1,384]{3,2,1,0:T(2,128)(2,1)S(1)} %get-tuple-element.102), channel_id=1, source_target_pairs={{1,0},{2,1},{3,2},{5,4},{6,5},{7,6},{9,8},{10,9},{11,10},{13,12},{... | collective-permute-start | bytes 27656 | tf_op jit(solution)/shard_map/ppermute | solution.py:21
  90.9 7.9 %collective-permute-start.8 = (bf16[2,6,1,384]{3,2,1,0:T(2,128)(2,1)S(1)}, bf16[2,6,1,384]{3,2,1,0:T(2,128)(2,1)S(1)}, u32[]{:S(2)}, u32[]{:S(2)}) collective-permute-start(bf16[2,6,1,384]{3,2,1,0:T(2,128)(2,1)S(1)} %get-tuple-element.103), channel_id=1, source_target_pairs={{0,1},{1,2},{2,3},{4,5},{5,6},{6,7},{8,9},{9,10},{10,11},{12,13},{... | collective-permute-start | bytes 27656 | tf_op jit(solution)/shard_map/ppermute | solution.py:20
  99.1 7.9 %slice-start.3 = ((s8[7962624]{0:T(1024)(128)(4,1)}), s8[4194304]{0:T(1024)(128)(4,1)S(1)}, s32[]{:S(2)}) async-start(s8[7962624]{0:T(1024)(128)(4,1)} %bitcast.403), calls=%async_computation.6 | async-start | bytes 8388608
  110.0 206.6 %copy-start.1 = (bf16[2,4,32,384]{3,2,1,0:T(8,128)(2,1)}, bf16[2,4,32,384]{3,2,1,0:T(8,128)(2,1)S(1)}, u32[]{:S(2)}) copy-start(bf16[2,4,32,384]{3,2,1,0:T(8,128)(2,1)S(1)} %slice.745) | copy-start | bytes 589828
  110.0 92.4 %collective-permute-start.9 = (bf16[2,4,32,384]{3,2,1,0:T(8,128)(2,1)S(1)}, bf16[2,4,32,384]{3,2,1,0:T(8,128)(2,1)S(1)}, u32[]{:S(2)}, u32[]{:S(2)}) collective-permute-start(bf16[2,4,32,384]{3,2,1,0:T(8,128)(2,1)S(1)} %slice.745), channel_id=1, source_target_pairs={{64,0},{128,64},{192,128},{65,1},{129,65},{193,129},{66,2},{130,66... | collective-permute-start | bytes 589832 | tf_op jit(solution)/shard_map/ppermute | solution.py:10
Sparse Core Ops, SparseCore 0:
  81.3 119.7 reduce-scatter.1
  203.5 110.8 all-reduce.2
where the time goes:
time: 324 us; the launch traced here: 323 us
  waiting for transfers between devices  210 us (65%)
  matrix products  56 us (17%)
  starting transfers between devices  33 us (10%)
  between operations  14.8 us (5%)
  other arithmetic  6.37 us (2%)
    psum x1, waiting for transfers between devices, body(): kernel_grad = lax.psum(owned, ('tm', 'width'))  111 us
    reduce_scatter x1, waiting for transfers between devices, body(): lax.psum_scatter(jnp.stack(pieces, 1).reshape(channels // lax.axis_size('...  87.3 us
    dot_general x27, matrix products, body(): lax.dot_general(scaled, block, (((0,), (0,)), ((), ())), preferred_elemen...  30.3 us
    dot_general x27, matrix products, body(): jnp.dot(block, kernel[:, tap_t, tap_h, tap_w, :], preferred_element_type=...  17.2 us
    ppermute x4, starting transfers between devices, with_halo(): before = lax.ppermute(last, axis, up)  15.6 us
    ppermute x2, starting transfers between devices, shifted(): return lax.ppermute(value, axis, pairs)  12.1 us
    ppermute x4, waiting for transfers between devices, with_halo(): after = lax.ppermute(initial, axis, down)  8.73 us
    dot_general x27, matrix products, body(): lax.dot_general(block, kernel[:, tap_t, tap_h, tap_w, :], (((1,), (1,)),...  8.56 us
  transfers between devices with their start and end apart: 12, of which 6 were waited for; matrix products, arithmetic and copies ran while one was open for 6% of the time, Pallas kernels for 0%

commit v1 on v0

--- a/solution.py
+++ b/solution.py
@@ -96,7 +96,7 @@
         scatter_dimension=0,
         tiled=True,
     )
-    kernel_grad = lax.psum(owned, ("tm", "width"))
+    kernel_grad = jnp.sum(lax.all_gather(owned, ("tm", "width")), axis=0)
     return (decoded, frame_grad, cache_grad, kernel_grad)
 
 

time: 324 us -> 475 us (1.47)
  waiting for transfers between devices: 210 us -> 354 us
  other arithmetic: 6.37 us -> 13.7 us
    all_gather x0 -> x1, waiting for transfers between devices: none -> 211 us  [body(): kernel_grad = jnp.sum(lax.all_gather(owned, ('tm', 'width')), axis=0)]
    psum x1 -> x0, waiting for transfers between devices: 111 us -> none  [body(): kernel_grad = lax.psum(owned, ('tm', 'width'))]
    reduce_scatter x1, waiting for transfers between devices: 87.3 us -> 120 us  [body(): lax.psum_scatter(jnp.stack(pieces, 1).reshape(channels // lax.axis_size('...]
    ppermute x2, waiting for transfers between devices: 2.89 us -> 13.7 us  [shifted(): return lax.ppermute(value, axis, pairs)]
    reduce_sum x0 -> x1, other arithmetic: none -> 7.36 us  [body(): kernel_grad = jnp.sum(lax.all_gather(owned, ('tm', 'width')), axis=0)]
  transfers between devices with their start and end apart: 12 -> 12, of which waited for: 6 -> 7; matrix products, arithmetic and copies ran while one was open for 6% -> 4% of each run, Pallas kernels for 0% -> 0%
where the time goes in v1:
time: 475 us; the launch traced here: 474 us
  waiting for transfers between devices  354 us (75%)
  matrix products  55.9 us (12%)
  starting transfers between devices  34.8 us (7%)
  between operations  14.8 us (3%)
  other arithmetic  13.7 us (3%)
    all_gather x1, waiting for transfers between devices, body(): kernel_grad = jnp.sum(lax.all_gather(owned, ('tm', 'width')), axis=0)  211 us
    reduce_scatter x1, waiting for transfers between devices, body(): lax.psum_scatter(jnp.stack(pieces, 1).reshape(channels // lax.axis_size('...  120 us
    dot_general x27, matrix products, body(): lax.dot_general(scaled, block, (((0,), (0,)), ((), ())), preferred_elemen...  30.3 us
    dot_general x27, matrix products, body(): jnp.dot(block, kernel[:, tap_t, tap_h, tap_w, :], preferred_element_type=...  17.1 us
    ppermute x2, starting transfers between devices, shifted(): return lax.ppermute(value, axis, pairs)  15.2 us
    ppermute x4, starting transfers between devices, with_halo(): before = lax.ppermute(last, axis, up)  14.4 us
    ppermute x2, waiting for transfers between devices, shifted(): return lax.ppermute(value, axis, pairs)  13.7 us
  transfers between devices with their start and end apart: 12, of which 7 were waited for; matrix products, arithmetic and copies ran while one was open for 4% of the time, Pallas kernels for 0%

profile of v1, /device:TPU:1, one launch (start us, length us, event | category | flops | bytes accessed | tf_op | source)
XLA Modules:
  0.0 473.8 jit_solution(3823915267147225844)
XLA Ops:
  7.2 10.2 %collective-permute-start = (bf16[2,4,32,384]{3,2,1,0:T(8,128)(2,1)}, bf16[2,4,32,384]{3,2,1,0:T(8,128)(2,1)S(1)}, u32[]{:S(2)}, u32[]{:S(2)}) collective-permute-start(bf16[2,4,32,384]{3,2,1,0:T(8,128)(2,1)} %param.15), channel_id=1, source_target_pairs={{0,64},{64,128},{128,192},{1,65},{65,129},{129,193},{2,66},{66,130... | collective-permute-start | bytes 589832 | tf_op jit(solution)/shard_map/ppermute | solution.py:10
  17.4 2.9 collective-permute-done
  21.2 3.2 collective-permute-start.1
  24.4 1.3 collective-permute-start.2
  26.7 3.1 collective-permute-done.2
  30.7 4.8 %collective-permute-start.3 = (bf16[4,6,1,384]{3,2,1,0:T(2,128)(2,1)S(1)}, bf16[4,6,1,384]{3,2,1,0:T(2,128)(2,1)S(1)}, u32[]{:S(2)}, u32[]{:S(2)}) collective-permute-start(bf16[4,6,1,384]{3,2,1,0:T(2,128)(2,1)S(1)} %get-tuple-element.80), channel_id=1, source_target_pairs={{0,1},{1,2},{2,3},{4,5},{5,6},{6,7},{8,9},{9,10},{10,11},{12,13},{... | collective-permute-start | bytes 55304 | tf_op jit(solution)/shard_map/ppermute | solution.py:20
  35.5 1.3 collective-permute-start.4
  36.8 1.1 pad_maximum_fusion.1
  38.1 2.1 collective-permute-done.4
  40.2 1.4 maximum_maximum_fusion
  52.0 1.1 fusion.25
  53.1 1.1 fusion.24
  54.3 1.1 fusion.23
  55.4 1.1 fusion.22
  56.5 1.1 fusion.21
  58.7 1.1 fusion.19
  59.8 1.1 fusion.18
  62.1 1.1 fusion.16
  65.4 1.2 fusion.13
  66.6 1.2 fusion.12
  70.0 1.1 fusion.9
  71.1 1.1 fusion.8
  72.2 1.1 fusion.7
  73.3 1.1 fusion.6
  74.4 1.2 fusion.5
  77.8 1.1 fusion.2
  78.9 1.1 fusion.1
  80.0 1.1 fusion
  81.2 119.9 %reduce-scatter.2.cloned.1.call-done = f32[24,3,3,3,384]{4,0,3,2,1:T(8,128)} async-done(((f32[384,3,3,3,384]{4,0,3,2,1:T(8,128)}), f32[24,3,3,3,384]{4,0,3,2,1:T(8,128)}) %reduce-scatter.2.cloned.1.call-update) | async-done | bytes 995344 | tf_op jit(solution)/shard_map/reduce_scatter | solution.py:91
  201.2 2.5 collective-permute-start.5
  203.7 1.3 collective-permute-start.6
  205.0 3.6 collective-permute-done.6
  208.7 1.3 collective-permute-start.7
  210.0 4.0 collective-permute-start.8
  214.0 1.3 fusion.70
  215.3 1.2 fusion.91
  216.5 1.2 fusion.50
  218.2 1.4 fusion.75
  219.5 1.2 convolution_add_fusion.20
  220.8 1.2 convolution_add_fusion.19
  222.0 1.2 convolution_add_fusion.18
  223.3 1.2 convolution_add_fusion.17
  224.5 1.2 convolution_add_fusion.16
  225.8 1.2 convolution_add_fusion.15
  229.7 5.0 %collective-permute-start.9 = (bf16[2,4,32,384]{3,2,1,0:T(8,128)(2,1)S(1)}, bf16[2,4,32,384]{3,2,1,0:T(8,128)(2,1)S(1)}, u32[]{:S(2)}, u32[]{:S(2)}) collective-permute-start(bf16[2,4,32,384]{3,2,1,0:T(8,128)(2,1)S(1)} %slice.745), channel_id=1, source_target_pairs={{64,0},{128,64},{192,128},{65,1},{129,65},{193,129},{66,2},{130,66... | collective-permute-start | bytes 589832 | tf_op jit(solution)/shard_map/ppermute | solution.py:10
  236.9 10.8 %collective-permute-done.9 = bf16[2,4,32,384]{3,2,1,0:T(8,128)(2,1)S(1)} collective-permute-done((bf16[2,4,32,384]{3,2,1,0:T(8,128)(2,1)S(1)}, bf16[2,4,32,384]{3,2,1,0:T(8,128)(2,1)S(1)}, u32[]{:S(2)}, u32[]{:S(2)}) %collective-permute-start.9) | collective-permute-done | bytes 196640 | tf_op jit(solution)/shard_map/ppermute | solution.py:10
  248.5 211.2 %all-gather.3.cloned.1.call-done = f32[384,3,3,3,384]{4,0,3,2,1:T(8,128)} async-done(((f32[24,3,3,3,384]{4,0,3,2,1:T(8,128)}), f32[384,3,3,3,384]{4,0,3,2,1:T(8,128)}) %all-gather.3.cloned.1.call-update) | async-done | bytes 15925264 | tf_op jit(solution)/shard_map/all_gather | solution.py:99
  459.6 7.4 %reduce_sum.9 = f32[24,3,3,3,384]{4,0,3,2,1:T(8,128)} reduce(f32[16,24,3,3,3,384]{5,1,0,4,3,2:T(8,128)} %bitcast.406, f32[]{:T(128)} %constant.126.clone.1), dimensions={0}, to_apply=%region_1.2 | reduce | flops 3732480 | bytes 16920580 | tf_op jit(solution)/shard_map/reduce_sum | solution.py:99
  (96 shorter events, 27.8 us)
Async XLA Ops:
  7.2 194.0 %reduce-scatter.2.cloned.1.call-start = ((), (), s32[]{:S(2)}) async-start(), calls=%async_computation.1 | async-start | bytes 16920576 | tf_op jit(solution)/shard_map/reduce_scatter | solution.py:91
  7.2 13.1 %collective-permute-start = (bf16[2,4,32,384]{3,2,1,0:T(8,128)(2,1)}, bf16[2,4,32,384]{3,2,1,0:T(8,128)(2,1)S(1)}, u32[]{:S(2)}, u32[]{:S(2)}) collective-permute-start(bf16[2,4,32,384]{3,2,1,0:T(8,128)(2,1)} %param.15), channel_id=1, source_target_pairs={{0,64},{64,128},{128,192},{1,65},{65,129},{129,193},{2,66},{66,130... | collective-permute-start | bytes 589832 | tf_op jit(solution)/shard_map/ppermute | solution.py:10
  17.4 24.6 %slice-start = ((s8[7962624]{0:T(1024)(128)(4,1)}), s8[4194304]{0:T(1024)(128)(4,1)S(1)}, s32[]{:S(2)}) async-start(s8[7962624]{0:T(1024)(128)(4,1)} %bitcast.402), calls=%async_computation.3 | async-start | bytes 8388608
  20.4 22.0 %copy-start.2 = (f32[384]{0:T(512)S(1)}, f32[384]{0:T(512)}, u32[]{:S(2)}) copy-start(f32[384]{0:T(512)} %param.18) | copy-start | bytes 4612
  21.2 5.4 %collective-permute-start.1 = (bf16[4,1,32,384]{3,2,1,0:T(8,128)(2,1)S(1)}, bf16[4,1,32,384]{3,2,1,0:T(8,128)(2,1)S(1)}, u32[]{:S(2)}, u32[]{:S(2)}) collective-permute-start(bf16[4,1,32,384]{3,2,1,0:T(8,128)(2,1)S(1)} %get-tuple-element.92), channel_id=1, source_target_pairs={{0,4},{4,8},{8,12},{12,16},{16,20},{20,24},{24,28},{28,32},{32,36}... | collective-permute-start | bytes 294920 | tf_op jit(solution)/shard_map/ppermute | solution.py:20
  24.4 5.4 %collective-permute-start.2 = (bf16[4,1,32,384]{3,2,1,0:T(8,128)(2,1)S(1)}, bf16[4,1,32,384]{3,2,1,0:T(8,128)(2,1)S(1)}, u32[]{:S(2)}, u32[]{:S(2)}) collective-permute-start(bf16[4,1,32,384]{3,2,1,0:T(8,128)(2,1)S(1)} %get-tuple-element.93), channel_id=1, source_target_pairs={{4,0},{8,4},{12,8},{16,12},{20,16},{24,20},{28,24},{32,28},{36,32}... | collective-permute-start | bytes 294920 | tf_op jit(solution)/shard_map/ppermute | solution.py:21
  30.7 7.4 %collective-permute-start.3 = (bf16[4,6,1,384]{3,2,1,0:T(2,128)(2,1)S(1)}, bf16[4,6,1,384]{3,2,1,0:T(2,128)(2,1)S(1)}, u32[]{:S(2)}, u32[]{:S(2)}) collective-permute-start(bf16[4,6,1,384]{3,2,1,0:T(2,128)(2,1)S(1)} %get-tuple-element.80), channel_id=1, source_target_pairs={{0,1},{1,2},{2,3},{4,5},{5,6},{6,7},{8,9},{9,10},{10,11},{12,13},{... | collective-permute-start | bytes 55304 | tf_op jit(solution)/shard_map/ppermute | solution.py:20
  35.5 4.7 collective-permute-start.4
  38.1 4.0 slice-start.1
  45.0 3.6 copy-start
  46.2 3.6 copy-start.3
  81.2 378.5 %all-gather.3.cloned.1.call-start = ((), (), s32[]{:S(2)}) async-start(), calls=%async_computation.2 | async-start | bytes 16920576 | tf_op jit(solution)/shard_map/all_gather | solution.py:99
  201.2 25.8 %slice-start.2 = ((s8[7962624]{0:T(1024)(128)(4,1)}), s8[3768320]{0:T(1024)(128)(4,1)S(1)}, s32[]{:S(2)}) async-start(s8[7962624]{0:T(1024)(128)(4,1)} %bitcast.404), calls=%async_computation.5 | async-start | bytes 7536640
  201.2 3.8 collective-permute-start.5
  203.7 4.9 %collective-permute-start.6 = (bf16[2,1,32,384]{3,2,1,0:T(8,128)(2,1)S(1)}, bf16[2,1,32,384]{3,2,1,0:T(8,128)(2,1)S(1)}, u32[]{:S(2)}, u32[]{:S(2)}) collective-permute-start(bf16[2,1,32,384]{3,2,1,0:T(8,128)(2,1)S(1)} %get-tuple-element.107), channel_id=1, source_target_pairs={{4,0},{8,4},{12,8},{16,12},{20,16},{24,20},{28,24},{32,28},{36,32}... | collective-permute-start | bytes 147464 | tf_op jit(solution)/shard_map/ppermute | solution.py:21
  208.7 9.1 %collective-permute-start.7 = (bf16[2,6,1,384]{3,2,1,0:T(2,128)(2,1)S(1)}, bf16[2,6,1,384]{3,2,1,0:T(2,128)(2,1)S(1)}, u32[]{:S(2)}, u32[]{:S(2)}) collective-permute-start(bf16[2,6,1,384]{3,2,1,0:T(2,128)(2,1)S(1)} %get-tuple-element.102), channel_id=1, source_target_pairs={{1,0},{2,1},{3,2},{5,4},{6,5},{7,6},{9,8},{10,9},{11,10},{13,12},{... | collective-permute-start | bytes 27656 | tf_op jit(solution)/shard_map/ppermute | solution.py:21
  210.0 7.8 %collective-permute-start.8 = (bf16[2,6,1,384]{3,2,1,0:T(2,128)(2,1)S(1)}, bf16[2,6,1,384]{3,2,1,0:T(2,128)(2,1)S(1)}, u32[]{:S(2)}, u32[]{:S(2)}) collective-permute-start(bf16[2,6,1,384]{3,2,1,0:T(2,128)(2,1)S(1)} %get-tuple-element.103), channel_id=1, source_target_pairs={{0,1},{1,2},{2,3},{4,5},{5,6},{6,7},{8,9},{9,10},{10,11},{12,13},{... | collective-permute-start | bytes 27656 | tf_op jit(solution)/shard_map/ppermute | solution.py:20
  218.1 8.9 %slice-start.3 = ((s8[7962624]{0:T(1024)(128)(4,1)}), s8[4194304]{0:T(1024)(128)(4,1)S(1)}, s32[]{:S(2)}) async-start(s8[7962624]{0:T(1024)(128)(4,1)} %bitcast.404), calls=%async_computation.6 | async-start | bytes 8388608
  229.7 237.3 %copy-start.1 = (bf16[2,4,32,384]{3,2,1,0:T(8,128)(2,1)}, bf16[2,4,32,384]{3,2,1,0:T(8,128)(2,1)S(1)}, u32[]{:S(2)}) copy-start(bf16[2,4,32,384]{3,2,1,0:T(8,128)(2,1)S(1)} %slice.745) | copy-start | bytes 589828
  229.7 18.0 %collective-permute-start.9 = (bf16[2,4,32,384]{3,2,1,0:T(8,128)(2,1)S(1)}, bf16[2,4,32,384]{3,2,1,0:T(8,128)(2,1)S(1)}, u32[]{:S(2)}, u32[]{:S(2)}) collective-permute-start(bf16[2,4,32,384]{3,2,1,0:T(8,128)(2,1)S(1)} %slice.745), channel_id=1, source_target_pairs={{64,0},{128,64},{192,128},{65,1},{129,65},{193,129},{66,2},{130,66... | collective-permute-start | bytes 589832 | tf_op jit(solution)/shard_map/ppermute | solution.py:10
Sparse Core Ops, SparseCore 0:
  81.3 119.8 reduce-scatter.1
  203.0 256.6 all-gather.2
